TPU v7x, 512 devices: a whole 4x4x16 slice. The times are simulated.
512 devices in a mesh: group: 16 (over y_lo, x, core), mp: 32 (over z, y_hi).
Axes of the slice: x: 4, y: 4 (y_hi: 2, y_lo: 2; y = y_hi * 2 + y_lo), z: 16, core: 2. Of those that a mesh axis runs over, the one named last changes fastest.
Arguments:
- arrivals: bfloat16 [65536, 2048], P(('group', 'mp')), may hold values from -6 to 6
- slots: int32 [65536], P(('group', 'mp')), may hold values from 0 to 4095, as said below
- lengths: int32 [16, 4], P('group'), may hold values from 1 to 3072, 4096 in all within a row
- w_joined: float32 [2048, 1536], P('mp', 'group')
- w_expand: float32 [512, 2048], P('mp', 'group'), may hold values from -0.25 to 0.25
Outputs:
- attended: bfloat16 [65536, 1024], P(('group', 'mp'))
Inputs may be any that keep to these rules, and one draw needn't show every extreme that they name: `slots`: within each group the entries form a permutation of 0 to 4095; the 128 entries of one device hold exactly 2 values of every aligned run of 64 values.
All inputs are finite; a program needn't handle non-finite values.
Results may differ from a plain program's by a relative error of at most 0.03.
The roundings to bfloat16 on the way count: a program that leaves them out, or rounds other values in their place, can miss the bound.
Values may be sent and summed in bfloat16 or wider, within the bound.
A program may use at most 64 MiB of HBM per device.

v0:
```python
import jax
import jax.numpy as jnp
from jax import lax
from jax.sharding import PartitionSpec as P

HEADS = 8
HDIM = 128


EPS = 1e-06
NEGATIVE = -1e30


def row_norm(values):
    mean_sq = jnp.mean(values * values, axis=-1, keepdims=True)
    return values * lax.rsqrt(mean_sq + EPS)


def segment_of(positions, ends):
    return jnp.sum((positions[..., None] >= ends).astype(jnp.int32), axis=-1)


def body(arrivals, slots, lengths, w_joined, w_expand):
    mp_count = lax.axis_size("mp")
    my_index = lax.axis_index("mp")
    shard_rows = arrivals.shape[0]
    half_rows = shard_rows // 2
    per_dest = shard_rows // mp_count
    width = arrivals.shape[1]
    qcols = HEADS * HDIM

    def position_of(owner, row_index):
        return owner * shard_rows + row_index

    dest_device = slots // shard_rows
    dest_row = slots % shard_rows
    send_order = jnp.argsort(dest_device * shard_rows + dest_row)
    sent = arrivals[send_order].reshape(mp_count, per_dest, width)
    sent_rows = dest_row[send_order].reshape(mp_count, per_dest)
    got, got_rows = (
        lax.all_to_all(sent, "mp", split_axis=0, concat_axis=0, tiled=True),
        lax.all_to_all(sent_rows, "mp", split_axis=0, concat_axis=0, tiled=True),
    )
    got_flat = got_rows.reshape(shard_rows)
    served = got.reshape(shard_rows, width)[jnp.argsort(got_flat)]
    normed = row_norm(served.astype(jnp.float32)).astype(jnp.bfloat16)
    joined_half = w_joined.astype(jnp.bfloat16)
    expand_half = w_expand.astype(jnp.bfloat16)
    joined_rows, expand_part = (
        lax.all_gather(joined_half, "group", axis=1, tiled=True),
        lax.all_gather(expand_half, "group", axis=1, tiled=True),
    )
    expand_full = lax.all_gather(expand_part, "mp", axis=0, tiled=True)
    proj = jnp.dot(
        normed,
        lax.all_gather(joined_rows, "mp", axis=0, tiled=True),
        preferred_element_type=jnp.float32,
    )
    query = (proj[:, :qcols] * HDIM ** (-0.5)).astype(jnp.bfloat16)
    latent = row_norm(proj[:, qcols:]).astype(jnp.bfloat16)
    query_split = query.reshape(2, half_rows, HEADS, HDIM)
    ends = jnp.cumsum(lengths[0])
    query_pos = position_of(my_index, lax.iota(jnp.int32, shard_rows)).reshape(2, half_rows)
    query_seg = segment_of(query_pos, ends)
    query_last = query_pos[:, -1]
    seg_first = query_seg[:, 0]
    seg_last = query_seg[:, -1]

    def absorb(state, sub_latent, key_pos, key_seg):
        peak, total, accum = state
        keyval = jnp.dot(sub_latent, expand_full, preferred_element_type=jnp.float32).astype(
            jnp.bfloat16
        )
        keyval = keyval.reshape(half_rows, HEADS, 2 * HDIM)
        scores = jnp.einsum(
            "aqhd,khd->ahqk", query_split, keyval[:, :, :HDIM], preferred_element_type=jnp.float32
        )
        allowed = (key_pos[None, None, :] <= query_pos[:, :, None]) & (
            key_seg[None, None, :] == query_seg[:, :, None]
        )
        allowed = allowed[:, None]
        masked = jnp.where(allowed, scores, NEGATIVE)
        new_peak = jnp.maximum(peak, jnp.max(masked, axis=-1))
        weights = jnp.where(allowed, jnp.exp(masked - new_peak[..., None]), 0.0)
        rescale = jnp.exp(peak - new_peak)
        total = total * rescale + jnp.sum(weights, axis=-1)
        update = jnp.einsum(
            "ahqk,khd->aqhd",
            weights.astype(jnp.bfloat16),
            keyval[:, :, HDIM:],
            preferred_element_type=jnp.float32,
        )
        accum = accum * jnp.transpose(rescale, (0, 2, 1))[..., None] + update
        return (new_peak, total, accum)

    start_state = (
        jnp.full((2, HEADS, half_rows), NEGATIVE, jnp.float32),
        jnp.zeros((2, HEADS, half_rows), jnp.float32),
        jnp.zeros((2, half_rows, HEADS, HDIM), jnp.float32),
    )
    rows_piece = lax.all_gather(latent, "mp", axis=0, tiled=True)
    sub_count = rows_piece.shape[0] // half_rows
    subs = rows_piece.reshape(sub_count, half_rows, rows_piece.shape[1])

    def visit(inner, inputs):
        sub_latent, sub_index = inputs
        first_key = sub_index * half_rows
        owner = first_key // shard_rows
        key_pos = position_of(owner, first_key % shard_rows + lax.iota(jnp.int32, half_rows))
        key_seg = segment_of(key_pos, ends)
        needed = jnp.any(
            (key_pos[0] <= query_last) & (key_seg[-1] >= seg_first) & (key_seg[0] <= seg_last)
        )
        updated = lax.cond(
            needed,
            lambda current: absorb(current, sub_latent, key_pos, key_seg),
            lambda current: current,
            inner,
        )
        return (updated, None)

    result, _ = lax.scan(visit, start_state, (subs, jnp.arange(sub_count, dtype=jnp.int32)))
    peak, total, accum = result
    outcome = (
        (accum / jnp.transpose(total, (0, 2, 1))[..., None])
        .reshape(shard_rows, qcols)
        .astype(jnp.bfloat16)
    )
    back = outcome[got_flat].reshape(mp_count, per_dest, qcols)
    returned = lax.all_to_all(back, "mp", split_axis=0, concat_axis=0, tiled=True).reshape(
        shard_rows, qcols
    )
    return returned[jnp.argsort(send_order)]


def solution(mesh):
    in_specs = (
        P(("group", "mp"), None),
        P(("group", "mp")),
        P("group", None),
        P("mp", "group"),
        P("mp", "group"),
    )
    out_specs = P(("group", "mp"), None)
    return jax.shard_map(body, mesh=mesh, in_specs=in_specs, out_specs=out_specs, check_vma=False)
```

profile of v0, /device:TPU:1, one launch (start us, length us, event | category | flops | bytes accessed | tf_op | source)
XLA Modules:
  0.0 1013.5 jit_solution(10872488785946122287)
XLA Ops:
  7.4 23.4 %all-gather = bf16[16,96,64]{1,2,0:T(8,128)(2,1)S(1)} all-gather(bf16[1,96,64]{1,2,0:T(8,128)(2,1)S(1)} %convert_bitcast_fusion), channel_id=1, replica_groups=mesh['group'=16,'mp'=32] {'group'}, dimensions={0}, use_global_device_ids=true | all-gather | bytes 208896 | tf_op jit(solution)/shard_map/all_gather | solution.py:50
  32.6 19.4 %all_gather.18 = bf16[16,2048]{1,0:T(8,128)(2,1)} all-gather(bf16[16,128]{1,0:T(8,128)(2,1)S(1)} %convert_element_type.52), channel_id=1, replica_groups=mesh['group'=16,'mp'=32] {'group'}, dimensions={1}, use_global_device_ids=true | all-gather | bytes 69632 | tf_op jit(solution)/shard_map/all_gather | solution.py:51
  52.8 2.5 sort.45
  57.2 14.3 %all-to-all-start.1 = ((s32[32,1,4]{2,1,0:T(1,128)}), s32[32,1,4]{2,1,0:T(1,128)S(1)}, u32[]{:S(2)}, u32[]{:S(2)}) async-start(s32[32,1,4]{2,1,0:T(1,128)} %bitcast.10), calls=%async_computation.1 | async-start | bytes 32768 | tf_op jit(solution)/shard_map/all_to_all | solution.py:42
  73.5 11.5 %all-to-all-done.1 = s32[32,1,4]{2,1,0:T(1,128)S(1)} async-done(((s32[32,1,4]{2,1,0:T(1,128)}), s32[32,1,4]{2,1,0:T(1,128)S(1)}, u32[]{:S(2)}, u32[]{:S(2)}) %all-to-all-start.1) | async-done | bytes 544 | tf_op jit(solution)/shard_map/all_to_all | solution.py:42
  85.0 3.9 all-to-all-start
  90.3 2.6 sort.46
  92.9 26.7 %all-to-all-done = bf16[32,4,2048]{2,1,0:T(4,128)(2,1)S(1)} async-done(((bf16[32,4,2048]{2,1,0:T(4,128)(2,1)}), bf16[32,4,2048]{2,1,0:T(4,128)(2,1)S(1)}, u32[]{:S(2)}, u32[]{:S(2)}) %all-to-all-start) | async-done | bytes 524320 | tf_op jit(solution)/shard_map/all_to_all | solution.py:41
  120.8 92.0 %all-gather.5.cloned.1.call-done = bf16[2048,1536]{1,0:T(8,128)(2,1)} async-done(((bf16[64,1536]{1,0:T(8,128)(2,1)}), bf16[2048,1536]{1,0:T(8,128)(2,1)}) %all-gather.5.cloned.1.call-update) | async-done | bytes 6291472 | tf_op jit(solution)/shard_map/all_gather | solution.py:56
  212.8 3.8 fusion.17
  218.4 141.4 %all-gather.9.cloned.1.call-done = bf16[512,2048]{1,0:T(8,128)(2,1)} async-done(((bf16[16,2048]{1,0:T(8,128)(2,1)}), bf16[512,2048]{1,0:T(8,128)(2,1)}) %all-gather.9.cloned.1.call-update) | async-done | bytes 2097168 | tf_op jit(solution)/shard_map/all_gather | solution.py:53
  359.8 162.6 %all-gather.7.cloned.1.call-done = bf16[4096,512]{1,0:T(8,128)(2,1)} async-done(((bf16[128,512]{1,0:T(8,128)(2,1)}), bf16[4096,512]{1,0:T(8,128)(2,1)}) %all-gather.7.cloned.1.call-update) | async-done | bytes 4194320 | tf_op jit(solution)/shard_map/all_gather | solution.py:101
  522.5 296.8 %while.17 = (s32[]{:T(128)}, f32[2,8,64]{2,0,1:T(2,128)S(1)}, f32[2,8,64]{2,0,1:T(2,128)S(1)}, f32[2,64,8,128]{3,1,0,2:T(8,128)S(1)}, s32[64]{0:T(128)S(1)}, /*i...) while((s32[]{:T(128)}, f32[2,8,64]{2,0,1:T(2,128)S(1)}, ...), condition=%wide.region_13.14_spmd.clone, body=%wide.region_6.13_spmd.clone.sunk | while | flops 168718304 | bytes 5937034 | solution.py:122
  524.4 1.9 and_reduce_fusion.2
  527.0 3.5 conditional.3
  527.2 2.1 convolution_convert_fusion
  532.4 1.9 and_reduce_fusion.2
  535.0 3.5 conditional.3
  535.2 2.1 convolution_convert_fusion
  540.4 1.9 and_reduce_fusion.2
  545.0 1.9 and_reduce_fusion.2
  549.5 1.9 and_reduce_fusion.2
  554.0 1.9 and_reduce_fusion.2
  558.5 1.9 and_reduce_fusion.2
  563.1 1.9 and_reduce_fusion.2
  567.6 1.9 and_reduce_fusion.2
  572.1 1.9 and_reduce_fusion.2
  576.7 1.9 and_reduce_fusion.2
  581.2 1.9 and_reduce_fusion.2
  585.7 1.9 and_reduce_fusion.2
  590.2 1.9 and_reduce_fusion.2
  594.8 1.9 and_reduce_fusion.2
  599.3 1.9 and_reduce_fusion.2
  603.8 1.9 and_reduce_fusion.2
  608.4 1.9 and_reduce_fusion.2
  612.9 1.9 and_reduce_fusion.2
  617.4 1.9 and_reduce_fusion.2
  621.9 1.9 and_reduce_fusion.2
  626.5 1.9 and_reduce_fusion.2
  631.0 1.9 and_reduce_fusion.2
  635.5 1.9 and_reduce_fusion.2
  640.1 1.9 and_reduce_fusion.2
  644.6 1.9 and_reduce_fusion.2
  649.1 1.9 and_reduce_fusion.2
  653.6 1.9 and_reduce_fusion.2
  658.2 1.9 and_reduce_fusion.2
  662.7 1.9 and_reduce_fusion.2
  667.2 1.9 and_reduce_fusion.2
  671.8 1.9 and_reduce_fusion.2
  676.3 1.9 and_reduce_fusion.2
  680.8 1.9 and_reduce_fusion.2
  685.3 1.9 and_reduce_fusion.2
  689.9 1.9 and_reduce_fusion.2
  694.4 1.9 and_reduce_fusion.2
  698.9 1.9 and_reduce_fusion.2
  703.5 1.9 and_reduce_fusion.2
  708.0 1.9 and_reduce_fusion.2
  712.5 1.9 and_reduce_fusion.2
  717.0 1.9 and_reduce_fusion.2
  721.6 1.9 and_reduce_fusion.2
  766.9 1.9 and_reduce_fusion.2
  821.4 167.4 %all-to-all-start.2 = ((bf16[32,4,1024]{2,1,0:T(4,128)(2,1)}), bf16[32,4,1024]{2,1,0:T(4,128)(2,1)S(1)}, u32[]{:S(2)}, u32[]{:S(2)}) async-start(bf16[32,4,1024]{2,1,0:T(4,128)(2,1)} %reshape.139), calls=%async_computation.2 | async-start | bytes 524288 | tf_op jit(solution)/shard_map/all_to_all | solution.py:130
  988.8 2.6 sort.47
  991.4 13.9 %all-to-all-done.2 = bf16[32,4,1024]{2,1,0:T(4,128)(2,1)S(1)} async-done(((bf16[32,4,1024]{2,1,0:T(4,128)(2,1)}), bf16[32,4,1024]{2,1,0:T(4,128)(2,1)S(1)}, u32[]{:S(2)}, u32[]{:S(2)}) %all-to-all-start.2) | async-done | bytes 262176 | tf_op jit(solution)/shard_map/all_to_all | solution.py:130
  (483 shorter events, 138.0 us)
Async XLA Ops:
  6.5 64.9 %copy-start = (bf16[128,2048]{1,0:T(8,128)(2,1)S(1)}, bf16[128,2048]{1,0:T(8,128)(2,1)}, u32[]{:S(2)}) copy-start(bf16[128,2048]{1,0:T(8,128)(2,1)} %param.9) | copy-start | bytes 1572868
  6.5 206.3 %all-gather.5.cloned.1.call-start = ((), (), s32[]{:S(2)}) async-start(), calls=%async_computation.3 | async-start | bytes 6488064 | tf_op jit(solution)/shard_map/all_gather | solution.py:56
  31.9 328.0 %all-gather.9.cloned.1.call-start = ((), (), s32[]{:S(2)}) async-start(), calls=%async_computation.5 | async-start | bytes 2162688 | tf_op jit(solution)/shard_map/all_gather | solution.py:53
  57.2 27.8 %all-to-all-start.1 = ((s32[32,1,4]{2,1,0:T(1,128)}), s32[32,1,4]{2,1,0:T(1,128)S(1)}, u32[]{:S(2)}, u32[]{:S(2)}) async-start(s32[32,1,4]{2,1,0:T(1,128)} %bitcast.10), calls=%async_computation.1 | async-start | bytes 32768 | tf_op jit(solution)/shard_map/all_to_all | solution.py:42
  85.0 34.6 %all-to-all-start = ((bf16[32,4,2048]{2,1,0:T(4,128)(2,1)}), bf16[32,4,2048]{2,1,0:T(4,128)(2,1)S(1)}, u32[]{:S(2)}, u32[]{:S(2)}) async-start(bf16[32,4,2048]{2,1,0:T(4,128)(2,1)} %reshape.133), calls=%async_computation | async-start | bytes 1048576 | tf_op jit(solution)/shard_map/all_to_all | solution.py:41
  88.9 433.5 %all-gather.7.cloned.1.call-start = ((), (), s32[]{:S(2)}) async-start(), calls=%async_computation.4 | async-start | bytes 4325376 | tf_op jit(solution)/shard_map/all_gather | solution.py:101
  120.8 96.7 %copy-start.1 = (s32[1,4]{1,0:T(1,128)S(1)}, s32[1,4]{1,0:T(1,128)}, u32[]{:S(2)}) copy-start(s32[1,4]{1,0:T(1,128)} %param.11) | copy-start | bytes 52
  821.4 184.0 %all-to-all-start.2 = ((bf16[32,4,1024]{2,1,0:T(4,128)(2,1)}), bf16[32,4,1024]{2,1,0:T(4,128)(2,1)S(1)}, u32[]{:S(2)}, u32[]{:S(2)}) async-start(bf16[32,4,1024]{2,1,0:T(4,128)(2,1)} %reshape.139), calls=%async_computation.2 | async-start | bytes 524288 | tf_op jit(solution)/shard_map/all_to_all | solution.py:130
Sparse Core Ops, SparseCore 0:
  32.0 180.8 all-gather.4
  215.9 143.8 all-gather.8
  362.9 159.4 all-gather.6
where the time goes:
time: 1030 us; the launch traced here: 1010 us
  waiting for transfers between devices  448 us (43%)
  starting transfers between devices  186 us (18%)
  other arithmetic  142 us (14%)
  local copies, waits for them, and re-layouts  86 us (8%)
  loops' own time  85.7 us (8%)
  blocking collectives  42.8 us (4%)
  between operations  13.3 us (1%)
    all_to_all x1, starting transfers between devices, body(): lax.all_to_all(back, 'mp', split_axis=0, concat_axis=0, tiled=True)  167 us
    all_gather x1, waiting for transfers between devices, body(): rows_piece = lax.all_gather(latent, 'mp', axis=0, tiled=True)  163 us
    all_gather x1, waiting for transfers between devices, body(): expand_full = lax.all_gather(expand_part, 'mp', axis=0, tiled=True)  141 us
    reduce_or x64, other arithmetic, visit(): jnp.any((key_pos[0] <= query_last) & (key_seg[-1] >= seg_first) & (key_se...  123 us
    all_gather x1, waiting for transfers between devices, body(): lax.all_gather(joined_rows, 'mp', axis=0, tiled=True)  92 us
    another operation x1, loops' own time, body(): lax.scan(visit, start_state, (subs, jnp.arange(sub_count, dtype=jnp.int32)))  84.8 us
    dynamic_slice x64, local copies, waits for them, and re-layouts, body(): lax.scan(visit, start_state, (subs, jnp.arange(sub_count, dtype=jnp.int32)))  37.6 us
    slice x64, local copies, waits for them, and re-layouts, visit(): key_seg[-1] >= seg_first  37.3 us
  transfers between devices with their start and end apart: 6, of which 6 were waited for; matrix products, arithmetic and copies ran while one was open for 2% of the time, Pallas kernels for 0%

commit v1 on v0

v1 whole, which is shorter than its diff:
```python
import functools

import jax
import jax.numpy as jnp
from jax import lax
from jax.experimental import pallas as pl
from jax.experimental.pallas import tpu as pltpu
from jax.sharding import PartitionSpec as P

HEADS = 8
HDIM = 128
QCOLS = HEADS * HDIM
RANK = 512
WIDTH = 2048
ROWS = 128
NZ = 16
JPART = 384
BLOCK = 256
EPS = 1e-06
NEGATIVE = -1e30
OPEN = 3e38
MESH = pl.DeviceIdType.MESH
LAST = (((1,), (1,)), ((), ()))


def kernel(
    arrivals_ref,
    slot_row_ref,
    slot_col_ref,
    lengths_ref,
    joined_ref,
    expand_ref,
    out_ref,
    wide,
    quad,
    full,
    proj,
    lat,
    kpos,
    absorbed,
    peak,
    total,
    acc,
    q_send,
    q_recv,
    z_send,
    z_recv,
    kz_send,
    kz_recv,
    y_send,
    y_recv,
    ky_send,
    ky_recv,
    x_send,
    x_recv,
    c_send,
    c_recv,
    h_send,
    h_recv,
    r_send,
    r_recv,
):
    g = lax.axis_index("group")
    m = lax.axis_index("mp")
    core, x, ylo = g % 2, (g // 2) % 4, g // 8
    z, yhi = m // 2, m % 2
    xl, xh = x % 2, x // 2
    y = yhi * 2 + ylo

    def group_of(ylo_, x_, core_):
        return (ylo_ * 4 + x_) * 2 + core_

    def mp_of(z_, yhi_):
        return z_ * 2 + yhi_

    def flip(value, bits, span):
        if span == 2:
            return (value + bits) % 2
        if bits == 2:
            return (value + 2) % 4
        low = value % 2
        if bits == 1:
            return value + 1 - 2 * low
        return 3 - value

    def y_peer(k):
        other = flip(y, k, 4)
        return (group_of(other % 2, x, core), mp_of(z, other // 2))

    def x_peer(k):
        return (group_of(ylo, flip(x, k, 4), core), m)

    core_peer = (group_of(ylo, x, 1 - core), m)
    diag_peer = (group_of(ylo, flip(x, 1, 4), 1 - core), m)
    half_peer = (g, mp_of(z, 1 - yhi))
    right = (g, mp_of((z + 1) % NZ, yhi))
    left = (g, mp_of((z + NZ - 1) % NZ, yhi))

    barrier = pltpu.get_barrier_semaphore()

    def greet(peer):
        pl.semaphore_signal(barrier, inc=1, device_id=peer, device_id_type=MESH)

    @pl.loop(1, NZ)
    def _(dz):
        greet((g, mp_of((z + dz) % NZ, yhi)))

    for k in (1, 2, 3):
        greet(y_peer(k))
        greet(x_peer(k))
    greet(core_peer)
    greet(diag_peer)

    def remote(src, dst, send, recv, peer):
        return pltpu.make_async_remote_copy(
            src_ref=src,
            dst_ref=dst,
            send_sem=send,
            recv_sem=recv,
            device_id=peer,
            device_id_type=MESH,
        )

    my_r = xl * 2 + core
    row_id = lax.broadcasted_iota(jnp.int32, (96, JPART), 0)
    col_id = lax.broadcasted_iota(jnp.int32, (96, JPART), 1)
    place = jnp.where(col_id == row_id + my_r * 96, 1.0, 0.0).astype(jnp.bfloat16)
    wide[...] = (
        jnp.dot(joined_ref[...].astype(jnp.bfloat16), place, preferred_element_type=jnp.float32)
        .astype(jnp.bfloat16)
        .reshape(4, 16, JPART)
    )
    kpos[z, yhi] = jnp.broadcast_to(slot_row_ref[...], (8, ROWS))
    quad[my_r] = wide[my_r]

    pl.semaphore_wait(barrier, 23)

    def quad_copy(k):
        pxl, pcore = (xl + k // 2) % 2, (core + k % 2) % 2
        peer = (group_of(ylo, xh * 2 + pxl, pcore), m)
        return remote(
            wide.at[pxl * 2 + pcore], quad.at[my_r], q_send.at[k], q_recv.at[k], peer
        )

    def quad_arrival(k):
        pxl, pcore = (xl + k // 2) % 2, (core + k % 2) % 2
        slot = pxl * 2 + pcore
        return remote(quad.at[slot], quad.at[slot], q_send.at[k], q_recv.at[k], core_peer)

    for k in (1, 2, 3):
        quad_copy(k).start()

    @pl.loop(1, NZ)
    def _(dz):
        peer = (g, mp_of((z + dz) % NZ, yhi))
        remote(kpos.at[z, yhi], kpos.at[z, yhi], kz_send.at[dz], kz_recv.at[dz], peer).start()

    for k in (1, 2, 3):
        quad_arrival(k).wait_recv()
    pieces = quad[...].astype(jnp.float32)
    mine = full.at[ylo, xh, z, yhi, xl, core]
    mine[:, :JPART] = (pieces[0] + pieces[1] + pieces[2] + pieces[3]).astype(jnp.bfloat16)
    mine[:, JPART:] = expand_ref[...].astype(jnp.bfloat16)

    @pl.loop(1, NZ)
    def _(dz):
        peer = (g, mp_of((z + dz) % NZ, yhi))
        remote(mine, mine, z_send.at[dz], z_recv.at[dz], peer).start()

    values = arrivals_ref[...].astype(jnp.float32)
    mean_sq = jnp.mean(values * values, axis=-1, keepdims=True)
    normed = (values * lax.rsqrt(mean_sq + EPS)).astype(jnp.bfloat16)

    @pl.loop(1, NZ)
    def _(dz):
        source = (z + NZ - dz) % NZ
        slot = full.at[ylo, xh, source, yhi, xl, core]
        remote(slot, slot, z_send.at[dz], z_recv.at[dz], right).wait_recv()
        keys = kpos.at[source, yhi]
        remote(keys, keys, kz_send.at[dz], kz_recv.at[dz], right).wait_recv()

    def y_copy(ylo_, yhi_, k, peer):
        part = full.at[ylo_, xh, :, yhi_, xl, core]
        return remote(part, part, y_send.at[k], y_recv.at[k], peer)

    for k in (1, 2, 3):
        y_copy(ylo, yhi, k, y_peer(k)).start()
    key_copy = remote(kpos.at[:, yhi], kpos.at[:, yhi], ky_send, ky_recv, half_peer)
    key_copy.start()
    for k in (1, 2, 3):
        other = flip(y, k, 4)
        y_copy(other % 2, other // 2, k, core_peer).wait_recv()

    def x_copy(x_, k, peer):
        part = full.at[:, x_ // 2, :, :, x_ % 2, core]
        return remote(part, part, x_send.at[k], x_recv.at[k], peer)

    for k in (1, 2, 3):
        x_copy(x, k, x_peer(k)).start()
    for k in (1, 2, 3):
        x_copy(flip(x, k, 4), k, core_peer).wait_recv()

    def c_copy(core_):
        part = full.at[:, :, :, :, :, core_]
        return remote(part, part, c_send, c_recv, core_peer)

    c_copy(core).start()
    c_copy(1 - core).wait_recv()

    for c in range(4):
        weight = full[c // 2, c % 2, :, :, :, :, :, 0:JPART].reshape(WIDTH, JPART)
        proj[:, c * JPART : (c + 1) * JPART] = jnp.dot(
            normed, weight, preferred_element_type=jnp.float32
        )
    raw = proj[:, QCOLS:]
    raw_sq = jnp.mean(raw * raw, axis=-1, keepdims=True)
    lat[z, yhi] = (raw * lax.rsqrt(raw_sq + EPS)).astype(jnp.bfloat16)

    def half_copy(yhi_):
        return remote(lat.at[z, yhi_], lat.at[z, yhi_], h_send, h_recv, half_peer)

    def ring_send(way, step, half):
        source = (z + NZ - step) % NZ if way == 0 else (z + step) % NZ
        block = lat.at[source, half]
        peer = right if way == 0 else left
        return remote(
            block, block, r_send.at[way, step, half], r_recv.at[way, step, half], peer
        )

    def ring_arrival(way, step, half):
        source = (z + 2 * NZ - 1 - step) % NZ if way == 0 else (z + 1 + step) % NZ
        block = lat.at[source, half]
        return remote(
            block, block, r_send.at[way, step, half], r_recv.at[way, step, half], right
        )

    half_copy(yhi).start()
    ring_send(0, 0, yhi).start()
    ring_send(1, 0, yhi).start()

    def expand_block(index):
        ylo_, x_, core_ = index // 8, (index // 2) % 4, index % 2
        return full[ylo_, x_ // 2, :, :, x_ % 2, core_, :, JPART:].reshape(RANK, HDIM)

    for h in range(HEADS):
        query = (proj[:, h * HDIM : (h + 1) * HDIM] * HDIM ** (-0.5)).astype(jnp.bfloat16)
        absorbed[h * ROWS : (h + 1) * ROWS, :] = lax.dot_general(
            query, expand_block(2 * h), LAST, preferred_element_type=jnp.float32
        ).astype(jnp.bfloat16)

    half_copy(1 - yhi).wait_recv()
    ring_send(0, 0, 1 - yhi).start()
    ring_send(1, 0, 1 - yhi).start()
    remote(kpos.at[:, 1 - yhi], kpos.at[:, 1 - yhi], ky_send, ky_recv, half_peer).wait_recv()

    query_pos = slot_col_ref[...]
    first = jnp.zeros_like(query_pos)
    end = lengths_ref[0, 0]
    for p in range(1, 4):
        first = jnp.where(query_pos >= end, end, first)
        end = end + lengths_ref[0, p]

    def limit_of(source):
        keys = jnp.concatenate([kpos[source, 0][0:1], kpos[source, 1][0:1]], axis=1)
        allowed = (keys <= query_pos) & (keys >= first)
        return jnp.where(allowed, OPEN, NEGATIVE)

    def attend(sources, start):
        limits = [limit_of(source) for source in sources]

        @pl.loop(0, HEADS * ROWS // BLOCK)
        def _(block):
            rows = pl.ds(pl.multiple_of(block * BLOCK, BLOCK), BLOCK)
            query = absorbed[rows, :]
            keys = [lat[source].reshape(2 * ROWS, RANK) for source in sources]
            scores = []
            for key, limit in zip(keys, limits):
                score = lax.dot_general(query, key, LAST, preferred_element_type=jnp.float32)
                score = jnp.minimum(score.reshape(BLOCK // ROWS, ROWS, 2 * ROWS), limit[None])
                scores.append(score.reshape(BLOCK, 2 * ROWS))
            top = functools.reduce(
                jnp.maximum, [jnp.max(score, axis=-1, keepdims=True) for score in scores]
            )
            if not start:
                old = peak[rows, :]
                top = jnp.maximum(old, top)
            weights = [jnp.exp(score - top) for score in scores]
            added = sum(jnp.sum(weight, axis=-1, keepdims=True) for weight in weights)
            update = sum(
                jnp.dot(weight.astype(jnp.bfloat16), key, preferred_element_type=jnp.float32)
                for weight, key in zip(weights, keys)
            )
            if start:
                total[rows, :] = added
                acc[rows, :] = update
            else:
                rescale = jnp.exp(old - top)
                total[rows, :] = total[rows, :] * rescale + added
                acc[rows, :] = acc[rows, :] * rescale + update
            peak[rows, :] = top

    attend([z], True)

    @pl.loop(0, 6)
    def _(step):
        for half in range(2):
            for way in range(2):
                ring_arrival(way, step, half).wait_recv()
                ring_send(way, step + 1, half).start()
        attend([(z + 2 * NZ - 1 - step) % NZ, (z + 1 + step) % NZ], False)

    for half in range(2):
        for way in range(2):
            ring_arrival(way, 6, half).wait_recv()
    for way in range(2):
        ring_send(way, 7, way).start()
    attend([(z + NZ - 7) % NZ, (z + 7) % NZ], False)
    for way in range(2):
        ring_arrival(way, 7, way).wait_recv()
    attend([(z + 8) % NZ], False)

    for h in range(HEADS):
        rows = slice(h * ROWS, (h + 1) * ROWS)
        mixed = (acc[rows, :] / total[rows, :]).astype(jnp.bfloat16)
        out_ref[:, h * HDIM : (h + 1) * HDIM] = jnp.dot(
            mixed, expand_block(2 * h + 1), preferred_element_type=jnp.float32
        ).astype(jnp.bfloat16)

    for k in (1, 2, 3):
        quad_copy(k).wait_send()
        y_copy(ylo, yhi, k, y_peer(k)).wait_send()
        x_copy(x, k, x_peer(k)).wait_send()

    @pl.loop(1, NZ)
    def _(dz):
        remote(mine, mine, z_send.at[dz], z_recv.at[dz], right).wait_send()
        keys = kpos.at[z, yhi]
        remote(keys, keys, kz_send.at[dz], kz_recv.at[dz], right).wait_send()

    key_copy.wait_send()
    c_copy(core).wait_send()
    half_copy(yhi).wait_send()

    @pl.loop(0, 7)
    def _(step):
        for half in range(2):
            for way in range(2):
                ring_send(way, step, half).wait_send()

    for way in range(2):
        ring_send(way, 7, way).wait_send()


def body(arrivals, slots, lengths, w_joined, w_expand):
    vmem = pl.BlockSpec(memory_space=pltpu.VMEM)
    smem = pl.BlockSpec(memory_space=pltpu.SMEM)
    dma = pltpu.SemaphoreType.DMA
    return pl.pallas_call(
        kernel,
        out_shape=jax.ShapeDtypeStruct((ROWS, QCOLS), jnp.bfloat16),
        in_specs=[vmem, vmem, vmem, smem, vmem, vmem],
        out_specs=vmem,
        scratch_shapes=[
            pltpu.VMEM((4, 16, JPART), jnp.bfloat16),
            pltpu.VMEM((4, 16, JPART), jnp.bfloat16),
            pltpu.VMEM((2, 2, NZ, 2, 2, 2, 16, JPART + HDIM), jnp.bfloat16),
            pltpu.VMEM((ROWS, QCOLS + RANK), jnp.float32),
            pltpu.VMEM((NZ, 2, ROWS, RANK), jnp.bfloat16),
            pltpu.VMEM((NZ, 2, 8, ROWS), jnp.int32),
            pltpu.VMEM((HEADS * ROWS, RANK), jnp.bfloat16),
            pltpu.VMEM((HEADS * ROWS, 1), jnp.float32),
            pltpu.VMEM((HEADS * ROWS, 1), jnp.float32),
            pltpu.VMEM((HEADS * ROWS, RANK), jnp.float32),
            dma((4,)),
            dma((4,)),
            dma((NZ,)),
            dma((NZ,)),
            dma((NZ,)),
            dma((NZ,)),
            dma((4,)),
            dma((4,)),
            dma,
            dma,
            dma((4,)),
            dma((4,)),
            dma,
            dma,
            dma,
            dma,
            dma((2, 8, 2)),
            dma((2, 8, 2)),
        ],
        compiler_params=pltpu.CompilerParams(
            collective_id=0, has_side_effects=True, vmem_limit_bytes=48 * 1024 * 1024
        ),
    )(
        arrivals,
        slots.reshape(1, ROWS),
        slots.reshape(ROWS, 1),
        lengths,
        w_joined,
        w_expand,
    )


def solution(mesh):
    in_specs = (
        P(("group", "mp"), None),
        P(("group", "mp")),
        P("group", None),
        P("mp", "group"),
        P("mp", "group"),
    )
    out_specs = P(("group", "mp"), None)
    return jax.shard_map(body, mesh=mesh, in_specs=in_specs, out_specs=out_specs, check_vma=False)
```

time: 1030 us -> 161 us (0.16); the launches traced: 1010 us -> 158 us
  waiting for transfers between devices: 448 us -> 0 us
  starting transfers between devices: 186 us -> 0 us
  Pallas kernels: 0 us -> 155 us
  other arithmetic: 142 us -> 0 us
  loops' own time: 85.7 us -> 0 us
  local copies, waits for them, and re-layouts: 86 us -> 3.16 us
  blocking collectives: 42.8 us -> 0 us
  between operations: 13.3 us -> 0.01 us
    all_gather x3 -> x0, waiting for transfers between devices: 396 us -> none  [the longest x1 163 us: body(): rows_piece = lax.all_gather(latent, 'mp', axis=0, tiled=True)]
    all_to_all x3 -> x0, starting transfers between devices: 186 us -> none  [the longest x1 167 us: body(): lax.all_to_all(back, 'mp', split_axis=0, concat_axis=0, tiled=True)]
    pallas_call x0 -> x1, Pallas kernels: none -> 155 us  [body(): pl.pallas_call(kernel, out_shape=jax.ShapeDtypeStruct((ROWS, QCOLS), jnp....]
    reduce_or x64 -> x0, other arithmetic: 123 us -> none  [visit(): jnp.any((key_pos[0] <= query_last) & (key_seg[-1] >= seg_first) & (key_se...]
    another operation x65 -> x0, loops' own time: 85.7 us -> none  [the longest x1 84.8 us: body(): lax.scan(visit, start_state, (subs, jnp.arange(sub_count, dtype=jnp.int32)))]
    all_to_all x3 -> x0, waiting for transfers between devices: 52.2 us -> none  [the longest x1 26.7 us: body(): lax.all_to_all(sent, 'mp', split_axis=0, concat_axis=0, tiled=True)]
    all_gather x2 -> x0, blocking collectives: 42.8 us -> none  [the longest x1 23.4 us: body(): lax.all_gather(joined_half, 'group', axis=1, tiled=True)]
    slice x67 -> x0, local copies, waits for them, and re-layouts: 37.6 us -> none  [the longest x64 37.3 us: visit(): key_seg[-1] >= seg_first]
  transfers between devices with their start and end apart: 6 -> 0, of which waited for: 6 -> 0; matrix products, arithmetic and copies ran while one was open for 2% -> 0% of each run, Pallas kernels for 0% -> 0%
where the time goes in v1:
time: 161 us; the launch traced here: 158 us
  Pallas kernels  155 us (96%)
  local copies, waits for them, and re-layouts  3.16 us (2%)
    pallas_call x1, Pallas kernels, body(): pl.pallas_call(kernel, out_shape=jax.ShapeDtypeStruct((ROWS, QCOLS), jnp....  155 us

profile of v1, /device:TPU:1, one launch (start us, length us, event | category | flops | bytes accessed | tf_op | source)
XLA Modules:
  0.0 157.9 jit_solution(10594663000547066365)
XLA Ops:
  0.0 0.0 copy-start.3
  0.0 0.7 copy-done.3
  0.7 0.0 copy-start.1
  0.7 0.0 copy-start.2
  0.7 0.0 copy-start.4
  0.7 0.1 copy.6.slot_col_ref
  0.8 0.6 copy-done.1
  1.4 0.0 copy-done.2
  1.4 0.0 copy-done.4
  1.4 0.0 copy-start
  1.4 1.0 copy-done
  2.5 154.8 %shard_map.55 = bf16[128,1024]{1,0:T(8,128)(2,1)S(1)} custom-call(bf16[128,2048]{1,0:T(8,128)(2,1)S(1)} %copy-done, s32[1,128]{1,0:T(1,128)S(1)} %bitcast.3, s32[128,1]{1,0:T(8,128)S(1)} %copy.6.slot_col_ref, s32[1,4]{1,0:T(1,128)S(1)} %copy-done.4, f32[64,96]{1,0:T(8,128)S(1)} %copy-done.1, f32[16,128]{1,0:T(8,128)S(1)} %copy-done.2), custom_call_target="tpu_custom_call" | custom-call | tf_op jit(solution)/shard_map/pallas_call | solution.py:358
  157.2 0.7 copy.8
Async XLA Ops:
  0.0 0.7 copy-start.3
  0.7 0.8 copy-start.1
  0.7 0.8 copy-start.2
  0.7 0.8 copy-start.4
  1.4 1.0 copy-start

commit v2 on v1

v2 whole, which is shorter than its diff:
```python
import functools

import jax
import jax.numpy as jnp
from jax import lax
from jax.experimental import pallas as pl
from jax.experimental.pallas import tpu as pltpu
from jax.sharding import PartitionSpec as P

HEADS = 8
HDIM = 128
QCOLS = HEADS * HDIM
RANK = 512
WIDTH = 2048
ROWS = 128
NZ = 16
NG = 16
SHARD = 96
QPART = 256
LPART = 128
KINDS = 3
ACROSS = ()
EPS = 1e-06
NEGATIVE = -1e30
OPEN = 3e38
MESH = pl.DeviceIdType.MESH
LAST = (((1,), (1,)), ((), ()))


def kernel(
    arrivals_ref,
    slot_row_ref,
    lengths_ref,
    joined_ref,
    expand_ref,
    out_ref,
    wide,
    shards,
    full_lat,
    full_map,
    full_query,
    query,
    lat,
    kpos,
    key_map,
    value_map,
    keys,
    values,
    peak,
    total,
    acc,
    g_send,
    g_recv,
    z_send,
    z_recv,
    kz_send,
    kz_recv,
    y_send,
    y_recv,
    ky_send,
    ky_recv,
    x_send,
    x_recv,
    c_send,
    c_recv,
    h_send,
    h_recv,
    r_send,
    r_recv,
    a_send,
    a_recv,
):
    g = lax.axis_index("group")
    m = lax.axis_index("mp")
    core, x, ylo = g % 2, (g // 2) % 4, g // 8
    z, yhi = m // 2, m % 2
    xl, xh = x % 2, x // 2
    y = yhi * 2 + ylo

    def group_of(ylo_, x_, core_):
        return (ylo_ * 4 + x_) * 2 + core_

    def mp_of(z_, yhi_):
        return z_ * 2 + yhi_

    def flip(value, bits, span):
        if span == 2:
            return (value + bits) % 2
        if bits == 2:
            return (value + 2) % 4
        low = value % 2
        if bits == 1:
            return value + 1 - 2 * low
        return 3 - value

    def y_peer(k):
        other = flip(y, k, 4)
        return (group_of(other % 2, x, core), mp_of(z, other // 2))

    def x_peer(k):
        return (group_of(ylo, flip(x, k, 4), core), m)

    core_peer = (group_of(ylo, x, 1 - core), m)
    half_peer = (g, mp_of(z, 1 - yhi))
    right = (g, mp_of((z + 1) % NZ, yhi))
    left = (g, mp_of((z + NZ - 1) % NZ, yhi))

    barrier = pltpu.get_barrier_semaphore()

    def greet(peer):
        pl.semaphore_signal(barrier, inc=1, device_id=peer, device_id_type=MESH)

    @pl.loop(1, NZ)
    def _(dz):
        greet((g, mp_of((z + dz) % NZ, yhi)))

    @pl.loop(1, NG)
    def _(k):
        greet(((g + k) % NG, m))

    greet(y_peer(2))
    greet(y_peer(3))

    def remote(src, dst, send, recv, peer):
        return pltpu.make_async_remote_copy(
            src_ref=src,
            dst_ref=dst,
            send_sem=send,
            recv_sem=recv,
            device_id=peer,
            device_id_type=MESH,
        )

    wide[...] = jnp.zeros_like(wide)
    wide[:, :, :SHARD] = joined_ref[...].astype(jnp.bfloat16).reshape(4, 16, SHARD)
    kpos[z, yhi] = jnp.broadcast_to(slot_row_ref[...], (8, ROWS))
    rows_at = g % 4
    part = g // 4
    shards[g] = wide[rows_at]

    def placing(first, count, start, width):
        row = lax.broadcasted_iota(jnp.int32, (count * HDIM, width), 0)
        col = lax.broadcasted_iota(jnp.int32, (count * HDIM, width), 1)
        inside = row % HDIM
        same = (inside < SHARD) & ((first + row // HDIM) * SHARD + inside == start + col)
        return jnp.where(same, 1.0, 0.0).astype(jnp.bfloat16)

    def placed(first, count, start, width):
        pieces = jnp.concatenate([shards[first + t] for t in range(count)], axis=1)
        return jnp.dot(
            pieces, placing(first, count, start, width), preferred_element_type=jnp.float32
        ).astype(jnp.bfloat16)

    pl.semaphore_wait(barrier, 32)

    @pl.loop(1, NG)
    def _(k):
        other = (g + k) % NG
        remote(
            wide.at[other % 4], shards.at[g], g_send.at[k], g_recv.at[k], (other, m)
        ).start()

    @pl.loop(1, NZ)
    def _(dz):
        peer = (g, mp_of((z + dz) % NZ, yhi))
        remote(kpos.at[z, yhi], kpos.at[z, yhi], kz_send.at[dz], kz_recv.at[dz], peer).start()

    @pl.loop(1, NG)
    def _(k):
        slot = shards.at[(g + NG - k) % NG]
        remote(slot, slot, g_send.at[k], g_recv.at[k], core_peer).wait_recv()

    fulls = (full_lat, full_map, full_query)

    def z_start(kind):
        @pl.loop(1, NZ)
        def _(dz):
            peer = (g, mp_of((z + dz) % NZ, yhi))
            mine = fulls[kind].at[ylo, xh, z, yhi, xl, core]
            remote(mine, mine, z_send.at[kind, dz], z_recv.at[kind, dz], peer).start()

    def z_wait(kind):
        @pl.loop(1, NZ)
        def _(dz):
            slot = fulls[kind].at[ylo, xh, (z + NZ - dz) % NZ, yhi, xl, core]
            remote(slot, slot, z_send.at[kind, dz], z_recv.at[kind, dz], right).wait_recv()

    lat_start = QCOLS + LPART * part
    full_lat[ylo, xh, z, yhi, xl, core] = placed(lat_start // SHARD, 2, lat_start, LPART)
    z_start(0)
    full_map[ylo, xh, z, yhi, xl, core] = expand_ref[...].astype(jnp.bfloat16)
    z_start(1)
    query_start = QPART * part
    full_query[ylo, xh, z, yhi, xl, core] = placed(query_start // SHARD, 4, query_start, QPART)
    z_start(2)

    def zs(half):
        return pl.ds(half * (NZ // 2), NZ // 2)

    def y_part(kind, half, y_, core_):
        if half == 0:
            return fulls[kind].at[y_ % 2, xh, zs(half), y_ // 2, xl, core_]
        return fulls[kind].at[y_ % 2, :, zs(half), y_ // 2, :, core_]

    def x_part(kind, half, x_, core_):
        if half == 0:
            return fulls[kind].at[:, x_ // 2, zs(half), :, x_ % 2, core_]
        return fulls[kind].at[ylo, x_ // 2, zs(half), yhi, x_ % 2, core_]

    def along(axis, kind, half, k):
        if axis == "y":
            block, peer, send, recv = y_part(kind, half, y, core), y_peer(k), y_send, y_recv
        else:
            block, peer, send, recv = x_part(kind, half, x, core), x_peer(k), x_send, x_recv
        return remote(block, block, send.at[kind, half, k], recv.at[kind, half, k], peer)

    def arrival(axis, kind, half, k):
        if axis == "y":
            block, send, recv = y_part(kind, half, flip(y, k, 4), core), y_send, y_recv
        else:
            block, send, recv = x_part(kind, half, flip(x, k, 4), core), x_send, x_recv
        return remote(block, block, send.at[kind, half, k], recv.at[kind, half, k], core_peer)

    order = (("y", "x"), ("x", "y"))

    def stage_start(kind, stage):
        for k in (1, 3, 2):
            for half in range(2):
                along(order[half][stage], kind, half, k).start()

    def stage_wait(kind, stage, half):
        for k in (1, 3, 2):
            arrival(order[half][stage], kind, half, k).wait_recv()

    def c_copy(kind, half, k, core_):
        if half == 0:
            block = x_part(kind, 0, flip(x, k, 4) if k else x, core_)
        else:
            block = y_part(kind, 1, flip(y, k, 4) if k else y, core_)
        return remote(
            block, block, c_send.at[kind, half, k], c_recv.at[kind, half, k], core_peer
        )

    def first_stage_end(kind):
        for half in range(2):
            stage_wait(kind, 0, half)
        stage_start(kind, 1)
        for half in range(2):
            c_copy(kind, half, 0, core).start()

    def second_stage_end(kind):
        for k in (1, 3, 2):
            for half in range(2):
                arrival(order[half][1], kind, half, k).wait_recv()
                c_copy(kind, half, k, core).start()

    def core_end(kind):
        for k in (0, 1, 3, 2):
            for half in range(2):
                c_copy(kind, half, k, 1 - core).wait_recv()

    rows_in = arrivals_ref[...].astype(jnp.float32)
    mean_sq = jnp.mean(rows_in * rows_in, axis=-1, keepdims=True)
    normed = (rows_in * lax.rsqrt(mean_sq + EPS)).astype(jnp.bfloat16)

    z_wait(0)
    stage_start(0, 0)
    first_stage_end(0)
    z_wait(1)
    stage_start(1, 0)
    z_wait(2)
    stage_start(2, 0)

    @pl.loop(1, NZ)
    def _(dz):
        block = kpos.at[(z + NZ - dz) % NZ, yhi]
        remote(block, block, kz_send.at[dz], kz_recv.at[dz], right).wait_recv()

    key_copy = remote(kpos.at[:, yhi], kpos.at[:, yhi], ky_send, ky_recv, half_peer)
    key_copy.start()
    second_stage_end(0)
    first_stage_end(1)
    core_end(0)

    raws = []
    for c in range(2):
        weight = jnp.concatenate(
            [full_lat[c, t].reshape(WIDTH, LPART) for t in range(2)], axis=1
        )
        raws.append(jnp.dot(normed, weight, preferred_element_type=jnp.float32))
    raw = jnp.concatenate(raws, axis=1)
    raw_sq = jnp.mean(raw * raw, axis=-1, keepdims=True)
    lat[z, yhi] = (raw * lax.rsqrt(raw_sq + EPS)).astype(jnp.bfloat16)

    def half_copy(yhi_):
        return remote(lat.at[z, yhi_], lat.at[z, yhi_], h_send, h_recv, half_peer)

    def ring_send(way, step, half):
        source = (z + NZ - step) % NZ if way == 0 else (z + step) % NZ
        block = lat.at[source, half]
        peer = right if way == 0 else left
        return remote(
            block, block, r_send.at[way, step, half], r_recv.at[way, step, half], peer
        )

    def ring_arrival(way, step, half):
        source = (z + 2 * NZ - 1 - step) % NZ if way == 0 else (z + 1 + step) % NZ
        block = lat.at[source, half]
        return remote(
            block, block, r_send.at[way, step, half], r_recv.at[way, step, half], right
        )

    def across(way, step, half):
        source = (z + 2 * NZ - 1 - step) % NZ if way == 0 else (z + 1 + step) % NZ
        block = lat.at[source, half]
        return remote(block, block, a_send.at[way, step], a_recv.at[way, step], half_peer)

    half_copy(yhi).start()
    ring_send(0, 0, yhi).start()
    ring_send(1, 0, yhi).start()
    half_copy(1 - yhi).wait_recv()
    if 0 not in ACROSS:
        ring_send(0, 0, 1 - yhi).start()
        ring_send(1, 0, 1 - yhi).start()
    remote(kpos.at[:, 1 - yhi], kpos.at[:, 1 - yhi], ky_send, ky_recv, half_peer).wait_recv()

    def pass_on(step):
        for way in range(2):
            ring_arrival(way, step, yhi).wait_recv()
            if step < 6:
                ring_send(way, step + 1, yhi).start()
            if step in ACROSS:
                across(way, step, yhi).start()
        for way in range(2):
            if step in ACROSS:
                across(way, step, 1 - yhi).wait_recv()
            else:
                ring_arrival(way, step, 1 - yhi).wait_recv()
            if step < 6 and step + 1 not in ACROSS:
                ring_send(way, step + 1, 1 - yhi).start()
        if step == 6:
            for way in range(2):
                ring_send(way, 7, way).start()

    first_stage_end(2)
    pass_on(0)
    second_stage_end(1)
    core_end(1)

    def expand_block(index):
        ylo_, x_, core_ = index // 8, (index // 2) % 4, index % 2
        return full_map[ylo_, x_ // 2, :, :, x_ % 2, core_].reshape(RANK, HDIM)

    eye_row = lax.broadcasted_iota(jnp.int32, (ROWS, ROWS), 0)
    eye_col = lax.broadcasted_iota(jnp.int32, (ROWS, ROWS), 1)
    diagonal = eye_row == eye_col
    eye = jnp.where(diagonal, 1.0, 0.0).astype(jnp.bfloat16)
    for h in range(HEADS):
        cols = slice(h * HDIM, (h + 1) * HDIM)
        key_map[:, cols] = expand_block(2 * h)
        value_map[cols, :] = lax.dot_general(
            eye, expand_block(2 * h + 1), LAST, preferred_element_type=jnp.float32
        ).astype(jnp.bfloat16)

    query_pos = slot_row_ref[...].astype(jnp.float32)
    slot_row = slot_row_ref[...]
    first = jnp.zeros_like(slot_row)
    end = lengths_ref[0, 0]
    for p in range(1, 4):
        first = jnp.where(slot_row >= end, end, first)
        end = end + lengths_ref[0, p]
    first = first.astype(jnp.float32)

    def widen(source):
        block = lat[source].reshape(2 * ROWS, RANK)
        keys[source] = jnp.dot(
            block, key_map[...], preferred_element_type=jnp.float32
        ).astype(jnp.bfloat16)
        values[source] = lax.dot_general(
            value_map[...], block, LAST, preferred_element_type=jnp.float32
        ).astype(jnp.bfloat16)

    def limit_of(source):
        limits = []
        for half in range(2):
            row = kpos[source, half][0:1].astype(jnp.float32)
            col = jnp.sum(jnp.where(diagonal, row, 0.0), axis=1, keepdims=True)
            allowed = (col <= query_pos) & (col >= first)
            limits.append(jnp.where(allowed, OPEN, NEGATIVE))
        return jnp.concatenate(limits, axis=0)

    def attend(sources, start):
        limits = [limit_of(source) for source in sources]
        for h in range(HEADS):
            cols = slice(h * HDIM, (h + 1) * HDIM)
            scores = [
                jnp.minimum(
                    lax.dot_general(
                        keys[source, :, cols],
                        query[:, cols],
                        LAST,
                        preferred_element_type=jnp.float32,
                    ),
                    limit,
                )
                for source, limit in zip(sources, limits)
            ]
            top = functools.reduce(
                jnp.maximum, [jnp.max(score, axis=0, keepdims=True) for score in scores]
            )
            if not start:
                old = peak[h]
                top = jnp.maximum(old, top)
            weights = [jnp.exp(score - top) for score in scores]
            added = sum(jnp.sum(weight, axis=0, keepdims=True) for weight in weights)
            update = sum(
                jnp.dot(
                    values[source, cols, :],
                    weight.astype(jnp.bfloat16),
                    preferred_element_type=jnp.float32,
                )
                for source, weight in zip(sources, weights)
            )
            if start:
                total[h] = added
                acc[h] = update
            else:
                rescale = jnp.exp(old - top)
                total[h] = total[h] * rescale + added
                acc[h] = acc[h] * rescale + update
            peak[h] = top

    def pair(step):
        return [(z + 2 * NZ - 1 - step) % NZ, (z + 1 + step) % NZ]

    def widen_pair(step):
        for source in pair(step):
            widen(source)

    widen(z)
    pass_on(1)
    widen_pair(0)
    pass_on(2)
    widen_pair(1)
    second_stage_end(2)
    pass_on(3)
    core_end(2)

    def project(c):
        weight = full_query[c // 2, c % 2].reshape(WIDTH, QPART)
        query[:, c * QPART : (c + 1) * QPART] = (
            jnp.dot(normed, weight, preferred_element_type=jnp.float32) * HDIM ** (-0.5)
        ).astype(jnp.bfloat16)

    project(0)
    project(1)
    widen_pair(2)
    pass_on(4)
    project(2)
    project(3)
    widen_pair(3)
    attend([z], True)
    attend(pair(0), False)
    pass_on(5)
    widen_pair(4)

    @pl.loop(1, 3)
    def _(step):
        attend(pair(step), False)

    pass_on(6)

    @pl.loop(5, 7)
    def _(step):
        widen_pair(step)

    @pl.loop(3, 7)
    def _(step):
        attend(pair(step), False)

    for way in range(2):
        ring_arrival(way, 7, way).wait_recv()
    widen((z + 8) % NZ)
    attend([(z + 8) % NZ], False)

    for h in range(HEADS):
        mixed = (acc[h] / total[h]).astype(jnp.bfloat16)
        out_ref[:, h * HDIM : (h + 1) * HDIM] = lax.dot_general(
            eye, mixed, LAST, preferred_element_type=jnp.float32
        ).astype(jnp.bfloat16)

    @pl.loop(1, NG)
    def _(k):
        remote(
            wide.at[(g + k) % 4], shards.at[g], g_send.at[k], g_recv.at[k], core_peer
        ).wait_send()

    @pl.loop(1, NZ)
    def _(dz):
        for kind in range(KINDS):
            mine = fulls[kind].at[ylo, xh, z, yhi, xl, core]
            remote(mine, mine, z_send.at[kind, dz], z_recv.at[kind, dz], right).wait_send()
        block = kpos.at[z, yhi]
        remote(block, block, kz_send.at[dz], kz_recv.at[dz], right).wait_send()

    key_copy.wait_send()
    for kind in range(KINDS):
        for half in range(2):
            for axis in ("x", "y"):
                for k in (1, 2, 3):
                    along(axis, kind, half, k).wait_send()
            for k in range(4):
                c_copy(kind, half, k, core).wait_send()
    half_copy(yhi).wait_send()

    for step in range(7):
        for way in range(2):
            ring_send(way, step, yhi).wait_send()
            if step in ACROSS:
                across(way, step, yhi).wait_send()
            else:
                ring_send(way, step, 1 - yhi).wait_send()

    for way in range(2):
        ring_send(way, 7, way).wait_send()


def body(arrivals, slots, lengths, w_joined, w_expand):
    vmem = pl.BlockSpec(memory_space=pltpu.VMEM)
    smem = pl.BlockSpec(memory_space=pltpu.SMEM)
    dma = pltpu.SemaphoreType.DMA
    return pl.pallas_call(
        kernel,
        out_shape=jax.ShapeDtypeStruct((ROWS, QCOLS), jnp.bfloat16),
        in_specs=[vmem, vmem, smem, vmem, vmem],
        out_specs=vmem,
        scratch_shapes=[
            pltpu.VMEM((4, 16, HDIM), jnp.bfloat16),
            pltpu.VMEM((NG, 16, HDIM), jnp.bfloat16),
            pltpu.VMEM((2, 2, NZ, 2, 2, 2, 16, LPART), jnp.bfloat16),
            pltpu.VMEM((2, 2, NZ, 2, 2, 2, 16, HDIM), jnp.bfloat16),
            pltpu.VMEM((2, 2, NZ, 2, 2, 2, 16, QPART), jnp.bfloat16),
            pltpu.VMEM((ROWS, QCOLS), jnp.bfloat16),
            pltpu.VMEM((NZ, 2, ROWS, RANK), jnp.bfloat16),
            pltpu.VMEM((NZ, 2, 8, ROWS), jnp.int32),
            pltpu.VMEM((RANK, QCOLS), jnp.bfloat16),
            pltpu.VMEM((QCOLS, RANK), jnp.bfloat16),
            pltpu.VMEM((NZ, 2 * ROWS, QCOLS), jnp.bfloat16),
            pltpu.VMEM((NZ, QCOLS, 2 * ROWS), jnp.bfloat16),
            pltpu.VMEM((HEADS, 1, ROWS), jnp.float32),
            pltpu.VMEM((HEADS, 1, ROWS), jnp.float32),
            pltpu.VMEM((HEADS, HDIM, ROWS), jnp.float32),
            dma((NG,)),
            dma((NG,)),
            dma((KINDS, NZ)),
            dma((KINDS, NZ)),
            dma((NZ,)),
            dma((NZ,)),
            dma((KINDS, 2, 4)),
            dma((KINDS, 2, 4)),
            dma,
            dma,
            dma((KINDS, 2, 4)),
            dma((KINDS, 2, 4)),
            dma((KINDS, 2, 4)),
            dma((KINDS, 2, 4)),
            dma,
            dma,
            dma((2, 8, 2)),
            dma((2, 8, 2)),
            dma((2, 8)),
            dma((2, 8)),
        ],
        compiler_params=pltpu.CompilerParams(
            collective_id=0, has_side_effects=True, vmem_limit_bytes=48 * 1024 * 1024
        ),
    )(
        arrivals,
        slots.reshape(1, ROWS),
        lengths,
        w_joined,
        w_expand,
    )


def solution(mesh):
    in_specs = (
        P(("group", "mp"), None),
        P(("group", "mp")),
        P("group", None),
        P("mp", "group"),
        P("mp", "group"),
    )
    out_specs = P(("group", "mp"), None)
    return jax.shard_map(body, mesh=mesh, in_specs=in_specs, out_specs=out_specs, check_vma=False)
```

time: 161 us -> 119 us (0.74); the launches traced: 158 us -> 119 us
  Pallas kernels: 155 us -> 115 us
    pallas_call x1, Pallas kernels: 155 us -> 115 us  [body(): pl.pallas_call(kernel, out_shape=jax.ShapeDtypeStruct((ROWS, QCOLS), jnp....]
where the time goes in v2:
time: 119 us
  Pallas kernels  115 us (97%)
  local copies, waits for them, and re-layouts  3.87 us (3%)
    pallas_call x1, Pallas kernels, body(): pl.pallas_call(kernel, out_shape=jax.ShapeDtypeStruct((ROWS, QCOLS), jnp....  115 us
    unnamed x11, local copies, waits for them, and re-layouts  3.87 us

profile of v2, /device:TPU:1, one launch (start us, length us, event | category | flops | bytes accessed | tf_op | source)
XLA Modules:
  0.0 118.5 jit_solution(18320862625527074989)
XLA Ops:
  0.0 0.0 copy-start.4
  0.0 0.0 copy-start.3
  0.0 0.7 copy-done.4
  0.7 0.0 copy-done.3
  0.7 0.0 copy-start
  0.7 1.0 copy-done
  1.7 0.0 copy-start.1
  1.7 0.8 copy-done.1
  2.5 0.0 copy-start.2
  2.5 0.7 copy-done.2
  3.2 114.6 %shard_map.55 = bf16[128,1024]{1,0:T(8,128)(2,1)S(1)} custom-call(bf16[128,2048]{1,0:T(8,128)(2,1)S(1)} %copy-done, s32[1,128]{1,0:T(1,128)S(1)} %bitcast.1, s32[1,4]{1,0:T(1,128)S(1)} %copy-done.4, f32[64,96]{1,0:T(8,128)S(1)} %copy-done.1, f32[16,128]{1,0:T(8,128)S(1)} %copy-done.2), custom_call_target="tpu_custom_call" | custom-call | tf_op jit(solution)/shard_map/pallas_call | solution.py:532
  117.8 0.7 copy.7
Async XLA Ops:
  0.0 0.7 copy-start.4
  0.0 0.7 copy-start.3
  0.7 1.0 copy-start
  1.7 0.8 copy-start.1
  2.5 0.7 copy-start.2

commit v3 on v2

--- a/solution.py
+++ b/solution.py
@@ -19,7 +19,7 @@
 QPART = 256
 LPART = 128
 KINDS = 3
-ACROSS = ()
+TOGETHER = 8
 EPS = 1e-06
 NEGATIVE = -1e30
 OPEN = 3e38
@@ -67,8 +67,6 @@
     h_recv,
     r_send,
     r_recv,
-    a_send,
-    a_recv,
 ):
     g = lax.axis_index("group")
     m = lax.axis_index("mp")
@@ -189,10 +187,8 @@
     full_lat[ylo, xh, z, yhi, xl, core] = placed(lat_start // SHARD, 2, lat_start, LPART)
     z_start(0)
     full_map[ylo, xh, z, yhi, xl, core] = expand_ref[...].astype(jnp.bfloat16)
-    z_start(1)
     query_start = QPART * part
     full_query[ylo, xh, z, yhi, xl, core] = placed(query_start // SHARD, 4, query_start, QPART)
-    z_start(2)
 
     def zs(half):
         return pl.ds(half * (NZ // 2), NZ // 2)
@@ -265,11 +261,11 @@
 
     z_wait(0)
     stage_start(0, 0)
+    z_start(1)
+    z_start(2)
     first_stage_end(0)
     z_wait(1)
     stage_start(1, 0)
-    z_wait(2)
-    stage_start(2, 0)
 
     @pl.loop(1, NZ)
     def _(dz):
@@ -279,7 +275,6 @@
     key_copy = remote(kpos.at[:, yhi], kpos.at[:, yhi], ky_send, ky_recv, half_peer)
     key_copy.start()
     second_stage_end(0)
-    first_stage_end(1)
     core_end(0)
 
     raws = []
@@ -310,41 +305,30 @@
             block, block, r_send.at[way, step, half], r_recv.at[way, step, half], right
         )
 
-    def across(way, step, half):
-        source = (z + 2 * NZ - 1 - step) % NZ if way == 0 else (z + 1 + step) % NZ
-        block = lat.at[source, half]
-        return remote(block, block, a_send.at[way, step], a_recv.at[way, step], half_peer)
-
     half_copy(yhi).start()
     ring_send(0, 0, yhi).start()
     ring_send(1, 0, yhi).start()
+    first_stage_end(1)
+    z_wait(2)
+    stage_start(2, 0)
     half_copy(1 - yhi).wait_recv()
-    if 0 not in ACROSS:
-        ring_send(0, 0, 1 - yhi).start()
-        ring_send(1, 0, 1 - yhi).start()
+    ring_send(0, 0, 1 - yhi).start()
+    ring_send(1, 0, 1 - yhi).start()
     remote(kpos.at[:, 1 - yhi], kpos.at[:, 1 - yhi], ky_send, ky_recv, half_peer).wait_recv()
 
     def pass_on(step):
-        for way in range(2):
-            ring_arrival(way, step, yhi).wait_recv()
-            if step < 6:
-                ring_send(way, step + 1, yhi).start()
-            if step in ACROSS:
-                across(way, step, yhi).start()
-        for way in range(2):
-            if step in ACROSS:
-                across(way, step, 1 - yhi).wait_recv()
-            else:
-                ring_arrival(way, step, 1 - yhi).wait_recv()
-            if step < 6 and step + 1 not in ACROSS:
-                ring_send(way, step + 1, 1 - yhi).start()
+        for half in (yhi, 1 - yhi):
+            for way in range(2):
+                ring_arrival(way, step, half).wait_recv()
+                if step < 6:
+                    ring_send(way, step + 1, half).start()
         if step == 6:
             for way in range(2):
                 ring_send(way, 7, way).start()
 
-    first_stage_end(2)
     pass_on(0)
     second_stage_end(1)
+    first_stage_end(2)
     core_end(1)
 
     def expand_block(index):
@@ -391,9 +375,9 @@
 
     def attend(sources, start):
         limits = [limit_of(source) for source in sources]
-        for h in range(HEADS):
+        def scores_of(h):
             cols = slice(h * HDIM, (h + 1) * HDIM)
-            scores = [
+            return [
                 jnp.minimum(
                     lax.dot_general(
                         keys[source, :, cols],
@@ -405,6 +389,8 @@
                 )
                 for source, limit in zip(sources, limits)
             ]
+
+        def weigh(h, scores):
             top = functools.reduce(
                 jnp.maximum, [jnp.max(score, axis=0, keepdims=True) for score in scores]
             )
@@ -413,22 +399,31 @@
                 top = jnp.maximum(old, top)
             weights = [jnp.exp(score - top) for score in scores]
             added = sum(jnp.sum(weight, axis=0, keepdims=True) for weight in weights)
+            rescale = None
+            if start:
+                total[h] = added
+            else:
+                rescale = jnp.exp(old - top)
+                total[h] = total[h] * rescale + added
+            peak[h] = top
+            return [weight.astype(jnp.bfloat16) for weight in weights], rescale
+
+        def gather(h, weights, rescale):
+            cols = slice(h * HDIM, (h + 1) * HDIM)
             update = sum(
                 jnp.dot(
-                    values[source, cols, :],
-                    weight.astype(jnp.bfloat16),
-                    preferred_element_type=jnp.float32,
+                    values[source, cols, :], weight, preferred_element_type=jnp.float32
                 )
                 for source, weight in zip(sources, weights)
             )
-            if start:
-                total[h] = added
-                acc[h] = update
-            else:
-                rescale = jnp.exp(old - top)
-                total[h] = total[h] * rescale + added
-                acc[h] = acc[h] * rescale + update
-            peak[h] = top
+            acc[h] = update if start else acc[h] * rescale + update
+
+        for first_head in range(0, HEADS, TOGETHER):
+            heads = range(first_head, first_head + TOGETHER)
+            scored = [scores_of(h) for h in heads]
+            weighed = [weigh(h, scores) for h, scores in zip(heads, scored)]
+            for h, (weights, rescale) in zip(heads, weighed):
+                gather(h, weights, rescale)
 
     def pair(step):
         return [(z + 2 * NZ - 1 - step) % NZ, (z + 1 + step) % NZ]
@@ -437,13 +432,14 @@
         for source in pair(step):
             widen(source)
 
+    pass_on(1)
     widen(z)
-    pass_on(1)
     widen_pair(0)
     pass_on(2)
     widen_pair(1)
     second_stage_end(2)
     pass_on(3)
+    widen_pair(2)
     core_end(2)
 
     def project(c):
@@ -452,29 +448,27 @@
             jnp.dot(normed, weight, preferred_element_type=jnp.float32) * HDIM ** (-0.5)
         ).astype(jnp.bfloat16)
 
-    project(0)
-    project(1)
-    widen_pair(2)
+    for c in range(4):
+        project(c)
+    attend([z], True)
     pass_on(4)
-    project(2)
-    project(3)
     widen_pair(3)
-    attend([z], True)
-    attend(pair(0), False)
-    pass_on(5)
-    widen_pair(4)
-
-    @pl.loop(1, 3)
+
+    @pl.loop(0, 3)
     def _(step):
         attend(pair(step), False)
 
-    pass_on(6)
-
-    @pl.loop(5, 7)
+    pass_on(5)
+
+    @pl.loop(4, 6)
     def _(step):
         widen_pair(step)
-
-    @pl.loop(3, 7)
+        attend(pair(step - 1), False)
+
+    pass_on(6)
+    widen_pair(6)
+
+    @pl.loop(5, 7)
     def _(step):
         attend(pair(step), False)
 
@@ -513,13 +507,11 @@
                 c_copy(kind, half, k, core).wait_send()
     half_copy(yhi).wait_send()
 
-    for step in range(7):
-        for way in range(2):
-            ring_send(way, step, yhi).wait_send()
-            if step in ACROSS:
-                across(way, step, yhi).wait_send()
-            else:
-                ring_send(way, step, 1 - yhi).wait_send()
+    @pl.loop(0, 7)
+    def _(step):
+        for half in range(2):
+            for way in range(2):
+                ring_send(way, step, half).wait_send()
 
     for way in range(2):
         ring_send(way, 7, way).wait_send()
@@ -568,8 +560,6 @@
             dma,
             dma((2, 8, 2)),
             dma((2, 8, 2)),
-            dma((2, 8)),
-            dma((2, 8)),
         ],
         compiler_params=pltpu.CompilerParams(
             collective_id=0, has_side_effects=True, vmem_limit_bytes=48 * 1024 * 1024

time: 119 us -> 104 us (0.87)
  the two profiles are of different devices: /device:TPU:1 before, /device:TPU:24 now
where the time goes in v3:
time: 104 us
  Pallas kernels  100 us (96%)
  local copies, waits for them, and re-layouts  3.87 us (4%)
    pallas_call x1, Pallas kernels, body(): pl.pallas_call(kernel, out_shape=jax.ShapeDtypeStruct((ROWS, QCOLS), jnp....  100 us
    unnamed x11, local copies, waits for them, and re-layouts  3.87 us

profile of v3, /device:TPU:24, one launch (start us, length us, event | category | flops | bytes accessed | tf_op | source)
XLA Modules:
  0.0 104.0 jit_solution(5295491593214631485)
XLA Ops:
  0.0 0.0 copy-start.4
  0.0 0.0 copy-start.3
  0.0 0.7 copy-done.4
  0.7 0.0 copy-done.3
  0.7 0.0 copy-start
  0.7 1.0 copy-done
  1.7 0.0 copy-start.1
  1.7 0.8 copy-done.1
  2.5 0.0 copy-start.2
  2.5 0.7 copy-done.2
  3.2 100.1 %shard_map.55 = bf16[128,1024]{1,0:T(8,128)(2,1)S(1)} custom-call(bf16[128,2048]{1,0:T(8,128)(2,1)S(1)} %copy-done, s32[1,128]{1,0:T(1,128)S(1)} %bitcast.1, s32[1,4]{1,0:T(1,128)S(1)} %copy-done.4, f32[64,96]{1,0:T(8,128)S(1)} %copy-done.1, f32[16,128]{1,0:T(8,128)S(1)} %copy-done.2), custom_call_target="tpu_custom_call" | custom-call | tf_op jit(solution)/shard_map/pallas_call | solution.py:524
  103.2 0.7 copy.7
Async XLA Ops:
  0.0 0.7 copy-start.4
  0.0 0.7 copy-start.3
  0.7 1.0 %copy-start = (bf16[128,2048]{1,0:T(8,128)(2,1)S(1)}, bf16[128,2048]{1,0:T(8,128)(2,1)}, u32[]{:S(2)}) copy-start(bf16[128,2048]{1,0:T(8,128)(2,1)} %arrivals_ref.1) | copy-start | bytes 1572868
  1.7 0.8 copy-start.1
  2.5 0.7 copy-start.2

commit v4 on v3

--- a/solution.py
+++ b/solution.py
@@ -220,7 +220,7 @@
     order = (("y", "x"), ("x", "y"))
 
     def stage_start(kind, stage):
-        for k in (1, 3, 2):
+        for k in (2, 1, 3):
             for half in range(2):
                 along(order[half][stage], kind, half, k).start()
 

time: 104 us -> 102 us (0.981)
  the two profiles are of different devices: /device:TPU:24 before, /device:TPU:1 now
where the time goes in v4:
time: 102 us
  Pallas kernels  97.7 us (96%)
  local copies, waits for them, and re-layouts  3.87 us (4%)
    pallas_call x1, Pallas kernels, body(): pl.pallas_call(kernel, out_shape=jax.ShapeDtypeStruct((ROWS, QCOLS), jnp....  97.7 us
    unnamed x11, local copies, waits for them, and re-layouts  3.87 us

profile of v4, /device:TPU:1, one launch (start us, length us, event | category | flops | bytes accessed | tf_op | source)
XLA Modules:
  0.0 101.6 jit_solution(5866868013458210844)
XLA Ops:
  0.0 0.0 copy-start.4
  0.0 0.0 copy-start.3
  0.0 0.7 copy-done.4
  0.7 0.0 copy-done.3
  0.7 0.0 copy-start
  0.7 1.0 %copy-done = bf16[128,2048]{1,0:T(8,128)(2,1)S(1)} copy-done((bf16[128,2048]{1,0:T(8,128)(2,1)S(1)}, bf16[128,2048]{1,0:T(8,128)(2,1)}, u32[]{:S(2)}) %copy-start) | copy-done | bytes 524312
  1.7 0.0 copy-start.1
  1.7 0.8 copy-done.1
  2.5 0.0 copy-start.2
  2.5 0.7 copy-done.2
  3.2 97.7 %shard_map.55 = bf16[128,1024]{1,0:T(8,128)(2,1)S(1)} custom-call(bf16[128,2048]{1,0:T(8,128)(2,1)S(1)} %copy-done, s32[1,128]{1,0:T(1,128)S(1)} %bitcast.1, s32[1,4]{1,0:T(1,128)S(1)} %copy-done.4, f32[64,96]{1,0:T(8,128)S(1)} %copy-done.1, f32[16,128]{1,0:T(8,128)S(1)} %copy-done.2), custom_call_target="tpu_custom_call" | custom-call | tf_op jit(solution)/shard_map/pallas_call | solution.py:524
  100.9 0.7 copy.7
Async XLA Ops:
  0.0 0.7 copy-start.4
  0.0 0.7 copy-start.3
  0.7 1.0 %copy-start = (bf16[128,2048]{1,0:T(8,128)(2,1)S(1)}, bf16[128,2048]{1,0:T(8,128)(2,1)}, u32[]{:S(2)}) copy-start(bf16[128,2048]{1,0:T(8,128)(2,1)} %arrivals_ref.1) | copy-start | bytes 1572868
  1.7 0.8 copy-start.1
  2.5 0.7 copy-start.2

commit v5 on v4

--- a/solution.py
+++ b/solution.py
@@ -22,7 +22,7 @@
 TOGETHER = 8
 EPS = 1e-06
 NEGATIVE = -1e30
-OPEN = 3e38
+OPEN = float("inf")
 MESH = pl.DeviceIdType.MESH
 LAST = (((1,), (1,)), ((), ()))
 
@@ -108,9 +108,12 @@
     def greet(peer):
         pl.semaphore_signal(barrier, inc=1, device_id=peer, device_id_type=MESH)
 
+    def distance(index):
+        return NZ // 2 + (index // 2) * (1 - 2 * (index % 2))
+
     @pl.loop(1, NZ)
-    def _(dz):
-        greet((g, mp_of((z + dz) % NZ, yhi)))
+    def _(index):
+        greet((g, mp_of((z + distance(index)) % NZ, yhi)))
 
     @pl.loop(1, NG)
     def _(k):
@@ -172,7 +175,8 @@
 
     def z_start(kind):
         @pl.loop(1, NZ)
-        def _(dz):
+        def _(index):
+            dz = distance(index)
             peer = (g, mp_of((z + dz) % NZ, yhi))
             mine = fulls[kind].at[ylo, xh, z, yhi, xl, core]
             remote(mine, mine, z_send.at[kind, dz], z_recv.at[kind, dz], peer).start()
@@ -465,24 +469,6 @@
         widen_pair(step)
         attend(pair(step - 1), False)
 
-    pass_on(6)
-    widen_pair(6)
-
-    @pl.loop(5, 7)
-    def _(step):
-        attend(pair(step), False)
-
-    for way in range(2):
-        ring_arrival(way, 7, way).wait_recv()
-    widen((z + 8) % NZ)
-    attend([(z + 8) % NZ], False)
-
-    for h in range(HEADS):
-        mixed = (acc[h] / total[h]).astype(jnp.bfloat16)
-        out_ref[:, h * HDIM : (h + 1) * HDIM] = lax.dot_general(
-            eye, mixed, LAST, preferred_element_type=jnp.float32
-        ).astype(jnp.bfloat16)
-
     @pl.loop(1, NG)
     def _(k):
         remote(
@@ -507,12 +493,33 @@
                 c_copy(kind, half, k, core).wait_send()
     half_copy(yhi).wait_send()
 
-    @pl.loop(0, 7)
+    @pl.loop(0, 6)
     def _(step):
         for half in range(2):
             for way in range(2):
                 ring_send(way, step, half).wait_send()
 
+    pass_on(6)
+    widen_pair(6)
+
+    @pl.loop(5, 7)
+    def _(step):
+        attend(pair(step), False)
+
+    for way in range(2):
+        ring_arrival(way, 7, way).wait_recv()
+    widen((z + 8) % NZ)
+    attend([(z + 8) % NZ], False)
+
+    for h in range(HEADS):
+        mixed = (acc[h] / total[h]).astype(jnp.bfloat16)
+        out_ref[:, h * HDIM : (h + 1) * HDIM] = lax.dot_general(
+            eye, mixed, LAST, preferred_element_type=jnp.float32
+        ).astype(jnp.bfloat16)
+
+    for half in range(2):
+        for way in range(2):
+            ring_send(way, 6, half).wait_send()
     for way in range(2):
         ring_send(way, 7, way).wait_send()
 

time: 102 us -> 102 us (level)
  no operation moved by 1% of the time
where the time goes in v5:
time: 102 us; the launch traced here: 101 us
  Pallas kernels  96.8 us (95%)
  local copies, waits for them, and re-layouts  3.87 us (4%)
    pallas_call x1, Pallas kernels, body(): pl.pallas_call(kernel, out_shape=jax.ShapeDtypeStruct((ROWS, QCOLS), jnp....  96.8 us
    unnamed x11, local copies, waits for them, and re-layouts  3.87 us

profile of v5, /device:TPU:1, one launch (start us, length us, event | category | flops | bytes accessed | tf_op | source)
XLA Modules:
  0.0 100.6 jit_solution(3515876085875271222)
XLA Ops:
  0.0 0.0 copy-start.4
  0.0 0.0 copy-start.3
  0.0 0.7 copy-done.4
  0.7 0.0 copy-done.3
  0.7 0.0 copy-start
  0.7 1.0 %copy-done = bf16[128,2048]{1,0:T(8,128)(2,1)S(1)} copy-done((bf16[128,2048]{1,0:T(8,128)(2,1)S(1)}, bf16[128,2048]{1,0:T(8,128)(2,1)}, u32[]{:S(2)}) %copy-start) | copy-done | bytes 524312
  1.7 0.0 copy-start.1
  1.7 0.8 copy-done.1
  2.5 0.0 copy-start.2
  2.5 0.7 copy-done.2
  3.2 96.8 %shard_map.55 = bf16[128,1024]{1,0:T(8,128)(2,1)S(1)} custom-call(bf16[128,2048]{1,0:T(8,128)(2,1)S(1)} %copy-done, s32[1,128]{1,0:T(1,128)S(1)} %bitcast.1, s32[1,4]{1,0:T(1,128)S(1)} %copy-done.4, f32[64,96]{1,0:T(8,128)S(1)} %copy-done.1, f32[16,128]{1,0:T(8,128)S(1)} %copy-done.2), custom_call_target="tpu_custom_call" | custom-call | tf_op jit(solution)/shard_map/pallas_call | solution.py:531
  99.9 0.7 copy.7
Async XLA Ops:
  0.0 0.7 copy-start.4
  0.0 0.7 copy-start.3
  0.7 1.0 %copy-start = (bf16[128,2048]{1,0:T(8,128)(2,1)S(1)}, bf16[128,2048]{1,0:T(8,128)(2,1)}, u32[]{:S(2)}) copy-start(bf16[128,2048]{1,0:T(8,128)(2,1)} %arrivals_ref.1) | copy-start | bytes 1572868
  1.7 0.8 copy-start.1
  2.5 0.7 copy-start.2
